TPU v7x, 256 devices: a whole 4x4x8 slice. The times are simulated.
256 devices in a mesh: freq: 16 (over z, core), seg: 16 (over x, y).
Axes of the slice: x: 4, y: 4, z: 8, core: 2. Of those that a mesh axis runs over, the one named last changes fastest.
Arguments:
- propagators: float32 [16, 256, 2, 128, 128], P('seg', 'freq'), may hold values from -2 to 2, as said below
- source_modes: float32 [256, 2, 128], P('freq'), may hold values from -6 to 6
Outputs:
- amplitudes: float32 [16, 256, 2, 128], P('seg', 'freq')
- waveforms: float32 [256, 16, 128], P('freq', 'seg')
Inputs may be any that keep to these rules, and one draw needn't show every extreme that they name: `propagators`: each propagator is a diagonal of unit phases times (the identity plus a dense complex coupling part).
All inputs are finite; a program needn't handle non-finite values.
Results may differ from a plain program's by a relative error of at most 0.00019.
Values sent between devices are 32-bit elements; how exact they have to be, the bound alone decides.
A program may use at most 64 MiB of HBM per device.

v0:
```python
import jax
import jax.numpy as jnp
from jax import lax
from jax.sharding import PartitionSpec as P


def split_up(array, dim, length):
    shape = array.shape
    pieces = array.reshape(*shape[:dim], length, shape[dim] // length, *shape[dim + 1 :])
    return jnp.moveaxis(pieces, dim, 0)


def sum_at_owner(array, axis, dim):
    pieces = split_up(array, dim, lax.axis_size(axis))
    arrived = lax.all_to_all(pieces, axis, split_axis=0, concat_axis=0, tiled=True)
    return arrived.sum(axis=0)


def apply_modes(prop, vec):
    hi = lax.Precision.HIGHEST
    real_part = jnp.einsum("fij,fj->fi", prop[:, 0], vec[:, 0], precision=hi) - jnp.einsum(
        "fij,fj->fi", prop[:, 1], vec[:, 1], precision=hi
    )
    imag_part = jnp.einsum("fij,fj->fi", prop[:, 0], vec[:, 1], precision=hi) + jnp.einsum(
        "fij,fj->fi", prop[:, 1], vec[:, 0], precision=hi
    )
    return jnp.stack([real_part, imag_part], axis=1)


def local(propagators, source_modes):
    own_prop = propagators[0]
    fr_count = own_prop.shape[0]
    seg_index = lax.axis_index("seg")
    seg_count = lax.axis_size("seg")
    group = (fr_count + seg_count - 1) // seg_count
    chain_props = lax.all_to_all(propagators, "seg", split_axis=1, concat_axis=0, tiled=True)
    my_src = lax.dynamic_slice_in_dim(source_modes, seg_index * group, group, 0)

    def advance(carry, prop):
        nxt = apply_modes(prop, carry)
        return (nxt, nxt)

    final_vec, chain_amps = lax.scan(advance, my_src, chain_props)
    returned = lax.all_to_all(chain_amps, "seg", split_axis=0, concat_axis=1, tiled=True)
    result = returned[0, :fr_count]
    total_times = lax.axis_size("freq") * fr_count
    freq_start = lax.axis_index("freq") * fr_count
    stacked = jnp.concatenate([result[:, 0], result[:, 1]], axis=0)
    scale = 1.0 / jnp.sqrt(jnp.float32(total_times))
    tgrid = jnp.arange(fr_count * lax.axis_size("freq"), dtype=jnp.int32)
    fgrid = freq_start + jnp.arange(fr_count, dtype=jnp.int32)
    phase = (tgrid[:, None] * fgrid[None, :] % total_times).astype(jnp.float32) * (
        2.0 * jnp.pi / total_times
    )
    table = jnp.concatenate([jnp.cos(phase), -jnp.sin(phase)], axis=1) * scale
    waveforms = sum_at_owner(
        jnp.dot(table, stacked, precision=lax.Precision.HIGHEST)[:, None, :], "freq", 0
    )
    return (result[None], waveforms)


def solution(mesh):
    placed = (P("seg", "freq", None, None, None), P("freq", None, None))
    return jax.shard_map(
        local,
        mesh=mesh,
        in_specs=placed,
        out_specs=(P("seg", "freq", None, None), P("freq", "seg", None)),
        check_vma=False,
    )
```

profile of v0, /device:TPU:1, one launch (start us, length us, event | category | flops | bytes accessed | tf_op | source)
XLA Modules:
  0.0 94.4 jit_solution(478646866631887296)
XLA Ops:
  0.6 7.6 %all-to-all-start = ((f32[1,16,2,128,128]{4,3,2,0,1:T(8,128)}), f32[1,16,2,128,128]{4,3,2,0,1:T(8,128)S(1)}, u32[]{:S(2)}, u32[]{:S(2)}) async-start(f32[1,16,2,128,128]{4,3,2,0,1:T(8,128)} %bitcast.95), calls=%async_computation | async-start | bytes 4194304 | tf_op jit(solution)/shard_map/all_to_all | solution.py:36
  8.3 27.8 %all-to-all-done = f32[1,16,2,128,128]{4,3,2,0,1:T(8,128)S(1)} async-done(((f32[1,16,2,128,128]{4,3,2,0,1:T(8,128)}), f32[1,16,2,128,128]{4,3,2,0,1:T(8,128)S(1)}, u32[]{:S(2)}, u32[]{:S(2)}) %all-to-all-start) | async-done | bytes 2097184 | tf_op jit(solution)/shard_map/all_to_all | solution.py:36
  36.1 23.7 %while.12 = (s32[]{:T(128)}, f32[1,2,128]{2,1,0:T(2,128)S(1)}, f32[16,1,2,128]{3,2,1,0:T(2,128)}, f32[16,1,2,128,128]{4,3,2,1,0:T(8,128)S(1)}, s32[]{:T(128)}) while((s32[]{:T(128)}, f32[1,2,128]{2,1,0:T(2,128)S(1)}, f32[16,1,2,128]{3,2,1,0:T(2,128)}, f32[16,1,2,128,128]{4,3,2,1,0:T(8,128)S(1)}, s32[]{:T(128)}) %tuple.33), condition=%wide.region_1.2_spmd, body=%wide.region_0.1_spmd.sunk | while | flops 786946 | bytes 533057 | solution.py:43
  36.3 0.2 fusion.40
  37.0 0.6 bitcast_dynamic-update-slice_fusion.2
  37.8 0.2 fusion.40
  38.2 0.2 fusion.39
  38.5 0.6 bitcast_dynamic-update-slice_fusion.2
  39.3 0.2 fusion.40
  39.7 0.2 fusion.39
  39.9 0.6 bitcast_dynamic-update-slice_fusion.2
  40.8 0.2 fusion.40
  41.4 0.6 bitcast_dynamic-update-slice_fusion.2
  42.9 0.6 bitcast_dynamic-update-slice_fusion.2
  44.4 0.6 bitcast_dynamic-update-slice_fusion.2
  45.9 0.6 bitcast_dynamic-update-slice_fusion.2
  47.3 0.6 bitcast_dynamic-update-slice_fusion.2
  48.8 0.6 bitcast_dynamic-update-slice_fusion.2
  50.3 0.6 bitcast_dynamic-update-slice_fusion.2
  51.8 0.6 bitcast_dynamic-update-slice_fusion.2
  53.3 0.6 bitcast_dynamic-update-slice_fusion.2
  54.7 0.6 bitcast_dynamic-update-slice_fusion.2
  56.2 0.6 bitcast_dynamic-update-slice_fusion.2
  57.7 0.6 bitcast_dynamic-update-slice_fusion.2
  59.2 0.6 bitcast_dynamic-update-slice_fusion.2
  59.8 3.9 %all-to-all-start.1 = ((f32[16,1,2,128]{3,2,1,0:T(2,128)}), f32[16,1,2,128]{3,2,1,0:T(2,128)S(1)}, u32[]{:S(2)}, u32[]{:S(2)}) async-start(f32[16,1,2,128]{3,2,1,0:T(2,128)} %get-tuple-element.24), calls=%async_computation.1 | async-start | bytes 32768 | tf_op jit(solution)/shard_map/all_to_all | solution.py:44
  63.9 6.3 %all-to-all-done.1 = f32[16,1,2,128]{3,2,1,0:T(2,128)S(1)} async-done(((f32[16,1,2,128]{3,2,1,0:T(2,128)}), f32[16,1,2,128]{3,2,1,0:T(2,128)S(1)}, u32[]{:S(2)}, u32[]{:S(2)}) %all-to-all-start.1) | async-done | bytes 16416 | tf_op jit(solution)/shard_map/all_to_all | solution.py:44
  70.2 1.0 %fusion.12 = f32[256,128]{1,0:T(8,128)} fusion(f32[256,16]{0,1:T(8,128)S(1)} %get-tuple-element.42, f32[256,16]{0,1:T(8,128)S(1)} %get-tuple-element.41, f32[16,128]{1,0:T(8,128)S(1)} %bitcast.99, f32[16,128]{1,0:T(8,128)S(1)} %bitcast.98), kind=kOutput, calls=%fused_computation.22 | convolution fusion | flops 12603392 | bytes 180224 | tf_op jit(solution)/shard_map/dot_general | solution.py:57
  71.2 12.8 %all-to-all-start.2 = ((f32[16,16,1,128]{3,1,2,0:T(8,128)}), f32[16,16,1,128]{3,1,2,0:T(8,128)S(1)}, u32[]{:S(2)}, u32[]{:S(2)}) async-start(f32[16,16,1,128]{3,1,2,0:T(8,128)} %bitcast.24), calls=%async_computation.2 | async-start | bytes 262144 | tf_op jit(solution)/shard_map/all_to_all | solution.py:15
  84.0 9.2 %all-to-all-done.2 = f32[16,16,1,128]{3,1,2,0:T(8,128)S(1)} async-done(((f32[16,16,1,128]{3,1,2,0:T(8,128)}), f32[16,16,1,128]{3,1,2,0:T(8,128)S(1)}, u32[]{:S(2)}, u32[]{:S(2)}) %all-to-all-start.2) | async-done | bytes 131104 | tf_op jit(solution)/shard_map/all_to_all | solution.py:15
  93.2 0.6 reduce_sum.11
  93.8 0.6 copy.24
  (81 shorter events, 12.5 us)
Async XLA Ops:
  0.6 7.7 %copy-start = (f32[16,2,128]{2,1,0:T(2,128)S(1)}, f32[16,2,128]{2,1,0:T(2,128)}, u32[]{:S(2)}) copy-start(f32[16,2,128]{2,1,0:T(2,128)} %param.5) | copy-start | bytes 49156
  0.6 35.5 %all-to-all-start = ((f32[1,16,2,128,128]{4,3,2,0,1:T(8,128)}), f32[1,16,2,128,128]{4,3,2,0,1:T(8,128)S(1)}, u32[]{:S(2)}, u32[]{:S(2)}) async-start(f32[1,16,2,128,128]{4,3,2,0,1:T(8,128)} %bitcast.95), calls=%async_computation | async-start | bytes 4194304 | tf_op jit(solution)/shard_map/all_to_all | solution.py:36
  59.8 10.4 %all-to-all-start.1 = ((f32[16,1,2,128]{3,2,1,0:T(2,128)}), f32[16,1,2,128]{3,2,1,0:T(2,128)S(1)}, u32[]{:S(2)}, u32[]{:S(2)}) async-start(f32[16,1,2,128]{3,2,1,0:T(2,128)} %get-tuple-element.24), calls=%async_computation.1 | async-start | bytes 32768 | tf_op jit(solution)/shard_map/all_to_all | solution.py:44
  71.2 21.9 %all-to-all-start.2 = ((f32[16,16,1,128]{3,1,2,0:T(8,128)}), f32[16,16,1,128]{3,1,2,0:T(8,128)S(1)}, u32[]{:S(2)}, u32[]{:S(2)}) async-start(f32[16,16,1,128]{3,1,2,0:T(8,128)} %bitcast.24), calls=%async_computation.2 | async-start | bytes 262144 | tf_op jit(solution)/shard_map/all_to_all | solution.py:15
where the time goes:
time: 94.7 us; the launch traced here: 94.4 us
  waiting for transfers between devices  43.3 us (46%)
  starting transfers between devices  24.3 us (26%)
  matrix products  14.5 us (15%)
  other arithmetic  10.7 us (11%)
    all_to_all x1, waiting for transfers between devices, local(): lax.all_to_all(propagators, 'seg', split_axis=1, concat_axis=0, tiled=True)  27.8 us
    all_to_all x1, starting transfers between devices, sum_at_owner(): lax.all_to_all(pieces, axis, split_axis=0, concat_axis=0, tiled=True)  12.8 us
    dynamic_update_slice x16, other arithmetic, local(): final_vec, chain_amps = lax.scan(advance, my_src, chain_props)  9.94 us
    all_to_all x1, waiting for transfers between devices, sum_at_owner(): lax.all_to_all(pieces, axis, split_axis=0, concat_axis=0, tiled=True)  9.17 us
    all_to_all x1, starting transfers between devices, local(): lax.all_to_all(propagators, 'seg', split_axis=1, concat_axis=0, tiled=True)  7.6 us
    all_to_all x1, waiting for transfers between devices, local(): lax.all_to_all(chain_amps, 'seg', split_axis=0, concat_axis=1, tiled=True)  6.29 us
    all_to_all x1, starting transfers between devices, local(): lax.all_to_all(chain_amps, 'seg', split_axis=0, concat_axis=1, tiled=True)  3.91 us
    dot_general x16, matrix products, apply_modes(): jnp.einsum('fij,fj->fi', prop[:, 1], vec[:, 1], precision=hi)  3.57 us
  transfers between devices with their start and end apart: 3, of which 3 were waited for; matrix products, arithmetic and copies ran while one was open for 0% of the time, Pallas kernels for 0%

commit v1 on v0

--- a/solution.py
+++ b/solution.py
@@ -41,7 +41,15 @@
         return (nxt, nxt)
 
     final_vec, chain_amps = lax.scan(advance, my_src, chain_props)
-    returned = lax.all_to_all(chain_amps, "seg", split_axis=0, concat_axis=1, tiled=True)
+    ways, here = (lax.axis_size("seg"), lax.axis_index("seg"))
+    width = chain_amps.shape[0] // ways
+    turned = jnp.roll(chain_amps, -here * width, axis=0)
+    got = [lax.slice_in_dim(turned, 0, width, axis=0)]
+    for far in range(1, ways):
+        sent = lax.slice_in_dim(turned, far * width, (far + 1) * width, axis=0)
+        got.append(lax.ppermute(sent, "seg", [(d, (d + far) % ways) for d in range(ways)]))
+    line = jnp.concatenate(got[::-1], axis=1)
+    returned = jnp.roll(line, (here + 1) * got[0].shape[1], axis=1)
     result = returned[0, :fr_count]
     total_times = lax.axis_size("freq") * fr_count
     freq_start = lax.axis_index("freq") * fr_count

time: 94.7 us -> 106 us (1.12)
  starting transfers between devices: 24.3 us -> 45.2 us
  other arithmetic: 10.7 us -> 1.71 us
  waiting for transfers between devices: 43.3 us -> 42.2 us
    ppermute x0 -> x15, starting transfers between devices: none -> 20.9 us  [local(): lax.ppermute(sent, 'seg', [(d, (d + far) % ways) for d in range(ways)])]
    dynamic_update_slice x16, other arithmetic: 9.94 us -> 0.87 us  [local(): final_vec, chain_amps = lax.scan(advance, my_src, chain_props)]
    all_to_all x1 -> x0, waiting for transfers between devices: 6.29 us -> none  [local(): lax.all_to_all(chain_amps, 'seg', split_axis=0, concat_axis=1, tiled=True)]
    ppermute x0 -> x15, waiting for transfers between devices: none -> 5.89 us  [local(): lax.ppermute(sent, 'seg', [(d, (d + far) % ways) for d in range(ways)])]
    all_to_all x1, starting transfers between devices: 12.8 us -> 16.7 us  [sum_at_owner(): lax.all_to_all(pieces, axis, split_axis=0, concat_axis=0, tiled=True)]
    all_to_all x1 -> x0, starting transfers between devices: 3.91 us -> none  [local(): lax.all_to_all(chain_amps, 'seg', split_axis=0, concat_axis=1, tiled=True)]
  transfers between devices with their start and end apart: 3 -> 17, of which waited for: 3 -> 5; matrix products, arithmetic and copies ran while one was open for 0% -> 1% of each run, Pallas kernels for 0% -> 0%
where the time goes in v1:
time: 106 us
  starting transfers between devices  45.2 us (43%)
  waiting for transfers between devices  42.2 us (40%)
  matrix products  14.5 us (14%)
  other arithmetic  1.71 us (2%)
    all_to_all x1, waiting for transfers between devices, local(): lax.all_to_all(propagators, 'seg', split_axis=1, concat_axis=0, tiled=True)  27.8 us
    ppermute x15, starting transfers between devices, local(): lax.ppermute(sent, 'seg', [(d, (d + far) % ways) for d in range(ways)])  20.9 us
    all_to_all x1, starting transfers between devices, sum_at_owner(): lax.all_to_all(pieces, axis, split_axis=0, concat_axis=0, tiled=True)  16.7 us
    all_to_all x1, waiting for transfers between devices, sum_at_owner(): lax.all_to_all(pieces, axis, split_axis=0, concat_axis=0, tiled=True)  8.54 us
    all_to_all x1, starting transfers between devices, local(): lax.all_to_all(propagators, 'seg', split_axis=1, concat_axis=0, tiled=True)  7.6 us
    ppermute x15, waiting for transfers between devices, local(): lax.ppermute(sent, 'seg', [(d, (d + far) % ways) for d in range(ways)])  5.89 us
    dot_general x16, matrix products, apply_modes(): jnp.einsum('fij,fj->fi', prop[:, 1], vec[:, 1], precision=hi)  3.57 us
    dot_general x16, matrix products, apply_modes(): jnp.einsum('fij,fj->fi', prop[:, 1], vec[:, 0], precision=hi)  3.57 us
  transfers between devices with their start and end apart: 17, of which 5 were waited for; matrix products, arithmetic and copies ran while one was open for 1% of the time, Pallas kernels for 0%

profile of v1, /device:TPU:1, one launch (start us, length us, event | category | flops | bytes accessed | tf_op | source)
XLA Modules:
  0.0 105.9 jit_solution(5714977669551232643)
XLA Ops:
  0.6 7.6 %all-to-all-start = ((f32[1,16,2,128,128]{4,3,2,0,1:T(8,128)}), f32[1,16,2,128,128]{4,3,2,0,1:T(8,128)S(1)}, u32[]{:S(2)}, u32[]{:S(2)}) async-start(f32[1,16,2,128,128]{4,3,2,0,1:T(8,128)} %bitcast.97), calls=%async_computation | async-start | bytes 4194304 | tf_op jit(solution)/shard_map/all_to_all | solution.py:36
  8.3 27.8 %all-to-all-done = f32[1,16,2,128,128]{4,3,2,0,1:T(8,128)S(1)} async-done(((f32[1,16,2,128,128]{4,3,2,0,1:T(8,128)}), f32[1,16,2,128,128]{4,3,2,0,1:T(8,128)S(1)}, u32[]{:S(2)}, u32[]{:S(2)}) %all-to-all-start) | async-done | bytes 2097184 | tf_op jit(solution)/shard_map/all_to_all | solution.py:36
  36.1 15.0 %while.12 = (s32[]{:T(128)}, f32[1,2,128]{2,1,0:T(2,128)S(1)}, f32[16,1,2,128]{3,2,1,0:T(2,128)S(1)}, f32[16,1,2,128,128]{4,3,2,1,0:T(8,128)S(1)}, s32[]{:T(128)}) while((s32[]{:T(128)}, f32[1,2,128]{2,1,0:T(2,128)S(1)}, f32[16,1,2,128]{3,2,1,0:T(2,128)S(1)}, f32[16,1,2,128,128]{4,3,2,1,0:T(8,128)S(1)}, s32[]{:T(128)}) %tuple.48), condition=%wide.region_1.2_spmd, body=%wide.region_0.1_spmd.sunk | while | flops 786946 | bytes 532549 | solution.py:43
  36.3 0.2 fusion.42
  37.3 0.2 fusion.42
  37.7 0.2 fusion.41
  38.2 0.2 fusion.42
  38.6 0.2 fusion.41
  39.1 0.2 fusion.42
  39.6 0.2 fusion.41
  51.3 0.5 collective-permute-start
  51.8 1.7 %collective-permute-start.1 = (f32[1,1,2,128]{3,1,2,0:T(1,128)S(1)}, f32[1,1,2,128]{3,1,2,0:T(1,128)S(1)}, u32[]{:S(2)}, u32[]{:S(2)}) collective-permute-start(f32[1,1,2,128]{3,1,2,0:T(1,128)S(1)} %get-tuple-element.59), channel_id=1, source_target_pairs={{0,14},{1,15},{2,0},{3,1},{4,2},{5,3},{6,4},{7,5},{8,6},{9,7},{10,... | collective-permute-start | bytes 3080 | tf_op jit(solution)/shard_map/ppermute | solution.py:50
  53.5 0.3 collective-permute-start.10
  53.8 1.5 %collective-permute-start.11 = (f32[1,1,2,128]{3,1,2,0:T(1,128)S(1)}, f32[1,1,2,128]{3,1,2,0:T(1,128)S(1)}, u32[]{:S(2)}, u32[]{:S(2)}) collective-permute-start(f32[1,1,2,128]{3,1,2,0:T(1,128)S(1)} %get-tuple-element.49), channel_id=1, source_target_pairs={{0,4},{1,5},{2,6},{3,7},{4,8},{5,9},{6,10},{7,11},{8,12},{9,13},{1... | collective-permute-start | bytes 3080 | tf_op jit(solution)/shard_map/ppermute | solution.py:50
  55.3 2.2 %collective-permute-start.12 = (f32[1,1,2,128]{3,1,2,0:T(1,128)S(1)}, f32[1,1,2,128]{3,1,2,0:T(1,128)S(1)}, u32[]{:S(2)}, u32[]{:S(2)}) collective-permute-start(f32[1,1,2,128]{3,1,2,0:T(1,128)S(1)} %get-tuple-element.48), channel_id=1, source_target_pairs={{0,3},{1,4},{2,5},{3,6},{4,7},{5,8},{6,9},{7,10},{8,11},{9,12},{10... | collective-permute-start | bytes 3080 | tf_op jit(solution)/shard_map/ppermute | solution.py:50
  57.5 0.8 collective-permute-start.13
  58.3 1.2 %collective-permute-done.10 = f32[1,1,2,128]{3,1,2,0:T(1,128)S(1)} collective-permute-done((f32[1,1,2,128]{3,1,2,0:T(1,128)S(1)}, f32[1,1,2,128]{3,1,2,0:T(1,128)S(1)}, u32[]{:S(2)}, u32[]{:S(2)}) %collective-permute-start.10) | collective-permute-done | bytes 1056 | tf_op jit(solution)/shard_map/ppermute | solution.py:50
  59.5 2.7 %collective-permute-start.2 = (f32[1,1,2,128]{3,1,2,0:T(1,128)S(1)}, f32[1,1,2,128]{3,1,2,0:T(1,128)S(1)}, u32[]{:S(2)}, u32[]{:S(2)}) collective-permute-start(f32[1,1,2,128]{3,1,2,0:T(1,128)S(1)} %get-tuple-element.58), channel_id=1, source_target_pairs={{0,13},{1,14},{2,15},{3,0},{4,1},{5,2},{6,3},{7,4},{8,5},{9,6},{10... | collective-permute-start | bytes 3080 | tf_op jit(solution)/shard_map/ppermute | solution.py:50
  62.3 1.5 %collective-permute-start.3 = (f32[1,1,2,128]{3,1,2,0:T(1,128)S(1)}, f32[1,1,2,128]{3,1,2,0:T(1,128)S(1)}, u32[]{:S(2)}, u32[]{:S(2)}) collective-permute-start(f32[1,1,2,128]{3,1,2,0:T(1,128)S(1)} %get-tuple-element.57), channel_id=1, source_target_pairs={{0,12},{1,13},{2,14},{3,15},{4,0},{5,1},{6,2},{7,3},{8,4},{9,5},{1... | collective-permute-start | bytes 3080 | tf_op jit(solution)/shard_map/ppermute | solution.py:50
  63.8 1.1 %collective-permute-start.4 = (f32[1,1,2,128]{3,1,2,0:T(1,128)S(1)}, f32[1,1,2,128]{3,1,2,0:T(1,128)S(1)}, u32[]{:S(2)}, u32[]{:S(2)}) collective-permute-start(f32[1,1,2,128]{3,1,2,0:T(1,128)S(1)} %get-tuple-element.56), channel_id=1, source_target_pairs={{0,11},{1,12},{2,13},{3,14},{4,15},{5,0},{6,1},{7,2},{8,3},{9,4},{... | collective-permute-start | bytes 3080 | tf_op jit(solution)/shard_map/ppermute | solution.py:50
  65.0 2.1 %collective-permute-start.5 = (f32[1,1,2,128]{3,1,2,0:T(1,128)S(1)}, f32[1,1,2,128]{3,1,2,0:T(1,128)S(1)}, u32[]{:S(2)}, u32[]{:S(2)}) collective-permute-start(f32[1,1,2,128]{3,1,2,0:T(1,128)S(1)} %get-tuple-element.55), channel_id=1, source_target_pairs={{0,10},{1,11},{2,12},{3,13},{4,14},{5,15},{6,0},{7,1},{8,2},{9,3},... | collective-permute-start | bytes 3080 | tf_op jit(solution)/shard_map/ppermute | solution.py:50
  67.1 1.9 %collective-permute-start.6 = (f32[1,1,2,128]{3,1,2,0:T(1,128)S(1)}, f32[1,1,2,128]{3,1,2,0:T(1,128)S(1)}, u32[]{:S(2)}, u32[]{:S(2)}) collective-permute-start(f32[1,1,2,128]{3,1,2,0:T(1,128)S(1)} %get-tuple-element.54), channel_id=1, source_target_pairs={{0,9},{1,10},{2,11},{3,12},{4,13},{5,14},{6,15},{7,0},{8,1},{9,2},... | collective-permute-start | bytes 3080 | tf_op jit(solution)/shard_map/ppermute | solution.py:50
  69.0 1.8 %collective-permute-start.7 = (f32[1,1,2,128]{3,1,2,0:T(1,128)S(1)}, f32[1,1,2,128]{3,1,2,0:T(1,128)S(1)}, u32[]{:S(2)}, u32[]{:S(2)}) collective-permute-start(f32[1,1,2,128]{3,1,2,0:T(1,128)S(1)} %get-tuple-element.53), channel_id=1, source_target_pairs={{0,8},{1,9},{2,10},{3,11},{4,12},{5,13},{6,14},{7,15},{8,0},{9,1},... | collective-permute-start | bytes 3080 | tf_op jit(solution)/shard_map/ppermute | solution.py:50
  70.8 1.2 %collective-permute-start.8 = (f32[1,1,2,128]{3,1,2,0:T(1,128)S(1)}, f32[1,1,2,128]{3,1,2,0:T(1,128)S(1)}, u32[]{:S(2)}, u32[]{:S(2)}) collective-permute-start(f32[1,1,2,128]{3,1,2,0:T(1,128)S(1)} %get-tuple-element.52), channel_id=1, source_target_pairs={{0,7},{1,8},{2,9},{3,10},{4,11},{5,12},{6,13},{7,14},{8,15},{9,0},... | collective-permute-start | bytes 3080 | tf_op jit(solution)/shard_map/ppermute | solution.py:50
  71.9 1.7 %collective-permute-start.9 = (f32[1,1,2,128]{3,1,2,0:T(1,128)S(1)}, f32[1,1,2,128]{3,1,2,0:T(1,128)S(1)}, u32[]{:S(2)}, u32[]{:S(2)}) collective-permute-start(f32[1,1,2,128]{3,1,2,0:T(1,128)S(1)} %get-tuple-element.51), channel_id=1, source_target_pairs={{0,6},{1,7},{2,8},{3,9},{4,10},{5,11},{6,12},{7,13},{8,14},{9,15},... | collective-permute-start | bytes 3080 | tf_op jit(solution)/shard_map/ppermute | solution.py:50
  73.6 2.0 %collective-permute-done.8 = f32[1,1,2,128]{3,1,2,0:T(1,128)S(1)} collective-permute-done((f32[1,1,2,128]{3,1,2,0:T(1,128)S(1)}, f32[1,1,2,128]{3,1,2,0:T(1,128)S(1)}, u32[]{:S(2)}, u32[]{:S(2)}) %collective-permute-start.8) | collective-permute-done | bytes 1056 | tf_op jit(solution)/shard_map/ppermute | solution.py:50
  75.6 2.7 %collective-permute-done.9 = f32[1,1,2,128]{3,1,2,0:T(1,128)S(1)} collective-permute-done((f32[1,1,2,128]{3,1,2,0:T(1,128)S(1)}, f32[1,1,2,128]{3,1,2,0:T(1,128)S(1)}, u32[]{:S(2)}, u32[]{:S(2)}) %collective-permute-start.9) | collective-permute-done | bytes 1056 | tf_op jit(solution)/shard_map/ppermute | solution.py:50
  78.4 1.0 fusion.12
  79.4 16.7 %all-to-all-start.1 = ((f32[16,16,1,128]{3,1,2,0:T(8,128)}), f32[16,16,1,128]{3,1,2,0:T(8,128)S(1)}, u32[]{:S(2)}, u32[]{:S(2)}) async-start(f32[16,16,1,128]{3,1,2,0:T(8,128)} %bitcast.25), calls=%async_computation.1 | async-start | bytes 262144 | tf_op jit(solution)/shard_map/all_to_all | solution.py:15
  96.2 0.6 copy.13
  96.8 8.5 %all-to-all-done.1 = f32[16,16,1,128]{3,1,2,0:T(8,128)S(1)} async-done(((f32[16,16,1,128]{3,1,2,0:T(8,128)}), f32[16,16,1,128]{3,1,2,0:T(8,128)S(1)}, u32[]{:S(2)}, u32[]{:S(2)}) %all-to-all-start.1) | async-done | bytes 131104 | tf_op jit(solution)/shard_map/all_to_all | solution.py:15
  105.3 0.6 reduce_sum.11
  (114 shorter events, 13.4 us)
Async XLA Ops:
  0.6 7.7 %copy-start = (f32[16,2,128]{2,1,0:T(2,128)S(1)}, f32[16,2,128]{2,1,0:T(2,128)}, u32[]{:S(2)}) copy-start(f32[16,2,128]{2,1,0:T(2,128)} %param.5) | copy-start | bytes 49156
  0.6 35.5 %all-to-all-start = ((f32[1,16,2,128,128]{4,3,2,0,1:T(8,128)}), f32[1,16,2,128,128]{4,3,2,0,1:T(8,128)S(1)}, u32[]{:S(2)}, u32[]{:S(2)}) async-start(f32[1,16,2,128,128]{4,3,2,0,1:T(8,128)} %bitcast.97), calls=%async_computation | async-start | bytes 4194304 | tf_op jit(solution)/shard_map/all_to_all | solution.py:36
  51.3 6.3 %collective-permute-start = (f32[1,1,2,128]{3,1,2,0:T(1,128)S(1)}, f32[1,1,2,128]{3,1,2,0:T(1,128)S(1)}, u32[]{:S(2)}, u32[]{:S(2)}) collective-permute-start(f32[1,1,2,128]{3,1,2,0:T(1,128)S(1)} %get-tuple-element.60), channel_id=1, source_target_pairs={{0,15},{1,0},{2,1},{3,2},{4,3},{5,4},{6,5},{7,6},{8,7},{9,8},{10,9... | collective-permute-start | bytes 3080 | tf_op jit(solution)/shard_map/ppermute | solution.py:50
  51.8 6.5 %collective-permute-start.1 = (f32[1,1,2,128]{3,1,2,0:T(1,128)S(1)}, f32[1,1,2,128]{3,1,2,0:T(1,128)S(1)}, u32[]{:S(2)}, u32[]{:S(2)}) collective-permute-start(f32[1,1,2,128]{3,1,2,0:T(1,128)S(1)} %get-tuple-element.59), channel_id=1, source_target_pairs={{0,14},{1,15},{2,0},{3,1},{4,2},{5,3},{6,4},{7,5},{8,6},{9,7},{10,... | collective-permute-start | bytes 3080 | tf_op jit(solution)/shard_map/ppermute | solution.py:50
  53.5 6.0 %collective-permute-start.10 = (f32[1,1,2,128]{3,1,2,0:T(1,128)S(1)}, f32[1,1,2,128]{3,1,2,0:T(1,128)S(1)}, u32[]{:S(2)}, u32[]{:S(2)}) collective-permute-start(f32[1,1,2,128]{3,1,2,0:T(1,128)S(1)} %get-tuple-element.50), channel_id=1, source_target_pairs={{0,5},{1,6},{2,7},{3,8},{4,9},{5,10},{6,11},{7,12},{8,13},{9,14},{... | collective-permute-start | bytes 3080 | tf_op jit(solution)/shard_map/ppermute | solution.py:50
  53.8 8.5 %collective-permute-start.11 = (f32[1,1,2,128]{3,1,2,0:T(1,128)S(1)}, f32[1,1,2,128]{3,1,2,0:T(1,128)S(1)}, u32[]{:S(2)}, u32[]{:S(2)}) collective-permute-start(f32[1,1,2,128]{3,1,2,0:T(1,128)S(1)} %get-tuple-element.49), channel_id=1, source_target_pairs={{0,4},{1,5},{2,6},{3,7},{4,8},{5,9},{6,10},{7,11},{8,12},{9,13},{1... | collective-permute-start | bytes 3080 | tf_op jit(solution)/shard_map/ppermute | solution.py:50
  55.3 8.5 %collective-permute-start.12 = (f32[1,1,2,128]{3,1,2,0:T(1,128)S(1)}, f32[1,1,2,128]{3,1,2,0:T(1,128)S(1)}, u32[]{:S(2)}, u32[]{:S(2)}) collective-permute-start(f32[1,1,2,128]{3,1,2,0:T(1,128)S(1)} %get-tuple-element.48), channel_id=1, source_target_pairs={{0,3},{1,4},{2,5},{3,6},{4,7},{5,8},{6,9},{7,10},{8,11},{9,12},{10... | collective-permute-start | bytes 3080 | tf_op jit(solution)/shard_map/ppermute | solution.py:50
  57.5 7.5 %collective-permute-start.13 = (f32[1,1,2,128]{3,1,2,0:T(1,128)S(1)}, f32[1,1,2,128]{3,1,2,0:T(1,128)S(1)}, u32[]{:S(2)}, u32[]{:S(2)}) collective-permute-start(f32[1,1,2,128]{3,1,2,0:T(1,128)S(1)} %get-tuple-element.47), channel_id=1, source_target_pairs={{0,2},{1,3},{2,4},{3,5},{4,6},{5,7},{6,8},{7,9},{8,10},{9,11},{10,... | collective-permute-start | bytes 3080 | tf_op jit(solution)/shard_map/ppermute | solution.py:50
  58.3 8.8 %collective-permute-start.14 = (f32[1,1,2,128]{3,1,2,0:T(1,128)S(1)}, f32[1,1,2,128]{3,1,2,0:T(1,128)S(1)}, u32[]{:S(2)}, u32[]{:S(2)}) collective-permute-start(f32[1,1,2,128]{3,1,2,0:T(1,128)S(1)} %get-tuple-element.46), channel_id=1, source_target_pairs={{0,1},{1,2},{2,3},{3,4},{4,5},{5,6},{6,7},{7,8},{8,9},{9,10},{10,1... | collective-permute-start | bytes 3080 | tf_op jit(solution)/shard_map/ppermute | solution.py:50
  59.5 9.4 %collective-permute-start.2 = (f32[1,1,2,128]{3,1,2,0:T(1,128)S(1)}, f32[1,1,2,128]{3,1,2,0:T(1,128)S(1)}, u32[]{:S(2)}, u32[]{:S(2)}) collective-permute-start(f32[1,1,2,128]{3,1,2,0:T(1,128)S(1)} %get-tuple-element.58), channel_id=1, source_target_pairs={{0,13},{1,14},{2,15},{3,0},{4,1},{5,2},{6,3},{7,4},{8,5},{9,6},{10... | collective-permute-start | bytes 3080 | tf_op jit(solution)/shard_map/ppermute | solution.py:50
  62.3 8.5 %collective-permute-start.3 = (f32[1,1,2,128]{3,1,2,0:T(1,128)S(1)}, f32[1,1,2,128]{3,1,2,0:T(1,128)S(1)}, u32[]{:S(2)}, u32[]{:S(2)}) collective-permute-start(f32[1,1,2,128]{3,1,2,0:T(1,128)S(1)} %get-tuple-element.57), channel_id=1, source_target_pairs={{0,12},{1,13},{2,14},{3,15},{4,0},{5,1},{6,2},{7,3},{8,4},{9,5},{1... | collective-permute-start | bytes 3080 | tf_op jit(solution)/shard_map/ppermute | solution.py:50
  63.8 8.2 %collective-permute-start.4 = (f32[1,1,2,128]{3,1,2,0:T(1,128)S(1)}, f32[1,1,2,128]{3,1,2,0:T(1,128)S(1)}, u32[]{:S(2)}, u32[]{:S(2)}) collective-permute-start(f32[1,1,2,128]{3,1,2,0:T(1,128)S(1)} %get-tuple-element.56), channel_id=1, source_target_pairs={{0,11},{1,12},{2,13},{3,14},{4,15},{5,0},{6,1},{7,2},{8,3},{9,4},{... | collective-permute-start | bytes 3080 | tf_op jit(solution)/shard_map/ppermute | solution.py:50
  65.0 8.6 %collective-permute-start.5 = (f32[1,1,2,128]{3,1,2,0:T(1,128)S(1)}, f32[1,1,2,128]{3,1,2,0:T(1,128)S(1)}, u32[]{:S(2)}, u32[]{:S(2)}) collective-permute-start(f32[1,1,2,128]{3,1,2,0:T(1,128)S(1)} %get-tuple-element.55), channel_id=1, source_target_pairs={{0,10},{1,11},{2,12},{3,13},{4,14},{5,15},{6,0},{7,1},{8,2},{9,3},... | collective-permute-start | bytes 3080 | tf_op jit(solution)/shard_map/ppermute | solution.py:50
  67.1 6.5 %collective-permute-start.6 = (f32[1,1,2,128]{3,1,2,0:T(1,128)S(1)}, f32[1,1,2,128]{3,1,2,0:T(1,128)S(1)}, u32[]{:S(2)}, u32[]{:S(2)}) collective-permute-start(f32[1,1,2,128]{3,1,2,0:T(1,128)S(1)} %get-tuple-element.54), channel_id=1, source_target_pairs={{0,9},{1,10},{2,11},{3,12},{4,13},{5,14},{6,15},{7,0},{8,1},{9,2},... | collective-permute-start | bytes 3080 | tf_op jit(solution)/shard_map/ppermute | solution.py:50
  69.0 4.7 %collective-permute-start.7 = (f32[1,1,2,128]{3,1,2,0:T(1,128)S(1)}, f32[1,1,2,128]{3,1,2,0:T(1,128)S(1)}, u32[]{:S(2)}, u32[]{:S(2)}) collective-permute-start(f32[1,1,2,128]{3,1,2,0:T(1,128)S(1)} %get-tuple-element.53), channel_id=1, source_target_pairs={{0,8},{1,9},{2,10},{3,11},{4,12},{5,13},{6,14},{7,15},{8,0},{9,1},... | collective-permute-start | bytes 3080 | tf_op jit(solution)/shard_map/ppermute | solution.py:50
  70.8 4.8 %collective-permute-start.8 = (f32[1,1,2,128]{3,1,2,0:T(1,128)S(1)}, f32[1,1,2,128]{3,1,2,0:T(1,128)S(1)}, u32[]{:S(2)}, u32[]{:S(2)}) collective-permute-start(f32[1,1,2,128]{3,1,2,0:T(1,128)S(1)} %get-tuple-element.52), channel_id=1, source_target_pairs={{0,7},{1,8},{2,9},{3,10},{4,11},{5,12},{6,13},{7,14},{8,15},{9,0},... | collective-permute-start | bytes 3080 | tf_op jit(solution)/shard_map/ppermute | solution.py:50
  71.9 6.3 %collective-permute-start.9 = (f32[1,1,2,128]{3,1,2,0:T(1,128)S(1)}, f32[1,1,2,128]{3,1,2,0:T(1,128)S(1)}, u32[]{:S(2)}, u32[]{:S(2)}) collective-permute-start(f32[1,1,2,128]{3,1,2,0:T(1,128)S(1)} %get-tuple-element.51), channel_id=1, source_target_pairs={{0,6},{1,7},{2,8},{3,9},{4,10},{5,11},{6,12},{7,13},{8,14},{9,15},... | collective-permute-start | bytes 3080 | tf_op jit(solution)/shard_map/ppermute | solution.py:50
  79.4 25.9 %all-to-all-start.1 = ((f32[16,16,1,128]{3,1,2,0:T(8,128)}), f32[16,16,1,128]{3,1,2,0:T(8,128)S(1)}, u32[]{:S(2)}, u32[]{:S(2)}) async-start(f32[16,16,1,128]{3,1,2,0:T(8,128)} %bitcast.25), calls=%async_computation.1 | async-start | bytes 262144 | tf_op jit(solution)/shard_map/all_to_all | solution.py:15
